TPU v7x, 256 devices: a whole 4x4x8 slice. The times are simulated.
256 devices in a mesh: blk: 32 (over x, z_lo, core), grp: 8 (over y, z_hi).
Axes of the slice: x: 4, y: 4, z: 8 (z_hi: 2, z_lo: 4; z = z_hi * 4 + z_lo), core: 2. Of those that a mesh axis runs over, the one named last changes fastest.
Arguments:
- activations: bfloat16 [16384, 8192], P('blk', 'grp'), may hold values from -6 to 6
- output_grads: bfloat16 [16384, 28672], P('blk', 'grp'), may hold values from -6 to 6
- query_left: bfloat16 [64, 32, 8192], P('blk', None, 'grp'), may hold values from -0.0078125 to 0.0078125
- query_right: bfloat16 [64, 32, 28672], P('blk', None, 'grp'), may hold values from -0.00390625 to 0.00390625
- basis_inputs: bfloat16 [32, 8192, 256], P('blk', 'grp'), may hold values from -0.0625 to 0.0625
- eigen_inputs: bfloat16 [32, 256], P('blk'), may hold values from 0.099609375 to 100
- basis_outputs: bfloat16 [32, 28672, 512], P('blk', 'grp'), may hold values from -0.03125 to 0.03125
- eigen_outputs: bfloat16 [32, 512], P('blk'), may hold values from 0.099609375 to 100
- owners: int32 [2], replicated, may hold values from 0 to 31
- seq_lengths: int32 [128], P('blk'), may hold values from 1 to 128, as said below
Outputs:
- scores: float32 [128, 64], P('blk')
Inputs may be any that keep to these rules, and one draw needn't show every extreme that they name: `seq_lengths`: the 4 lengths of one shard sum to at most 512; in every draw some shard is full (all its lengths 128) and some sequence has length 1.
All inputs are finite; a program needn't handle non-finite values.
Results may differ from a plain program's by a relative error of at most 0.02.
Values may be sent and summed in bfloat16 or wider, within the bound.
No kernel may reach another device: no remote copies, remote signals or barrier semaphores. Data moves between devices by JAX's collectives and lax.ppermute only.
A program may use at most 128 MiB of HBM per device.

v0:
```python
import jax
import jax.numpy as jnp
from jax import lax
from jax.sharding import PartitionSpec as P


def broadcast(x, axis, root):
    mine = lax.axis_index(axis) == root
    return lax.psum(jnp.where(mine, x, jnp.zeros_like(x)), axis)


def contract(row_block, factors):
    return lax.dot_general(
        row_block, factors, (((1,), (1,)), ((), ())), preferred_element_type=jnp.float32
    )


def finish(flat_rows, coeffs, basis, eigen):
    eigen_float = eigen.astype(jnp.float32)
    damped = (coeffs * (eigen_float / (1.0 + eigen_float))).astype(jnp.bfloat16)
    return (flat_rows.astype(jnp.float32) - contract(damped, basis)).astype(jnp.bfloat16)


def membership(seq_lens, slot_count):
    seq_ends = jnp.cumsum(seq_lens)
    seq_starts = seq_ends - seq_lens
    position = jnp.arange(slot_count, dtype=jnp.int32)[None, :]
    inside = (position >= seq_starts[:, None]) & (position < seq_ends[:, None])
    return inside.astype(jnp.float32)


def pair_scores(sum_left, sum_right, query_rank):
    product = (sum_left * sum_right).reshape(sum_left.shape[0], -1, query_rank)
    return jnp.sum(product, axis=2)


def local(
    activations,
    output_grads,
    query_left,
    query_right,
    basis_inputs,
    eigen_inputs,
    basis_outputs,
    eigen_outputs,
    owners,
    seq_lengths,
):
    basis_left, eigen_left = (
        broadcast(basis_inputs[0], "blk", owners[0]),
        broadcast(eigen_inputs[0], "blk", owners[0]),
    )
    basis_right, eigen_right = (
        broadcast(basis_outputs[0], "blk", owners[1]),
        broadcast(eigen_outputs[0], "blk", owners[1]),
    )
    query_rank = query_left.shape[1]
    left_flat = query_left.reshape(-1, query_left.shape[2])
    right_flat = query_right.reshape(-1, query_right.shape[2])
    left_coeffs = jnp.dot(left_flat, basis_left, preferred_element_type=jnp.float32)
    right_coeffs = jnp.dot(right_flat, basis_right, preferred_element_type=jnp.float32)
    left_coeffs, right_coeffs = (
        lax.psum(left_coeffs.astype(jnp.bfloat16), "grp").astype(jnp.float32),
        lax.psum(right_coeffs.astype(jnp.bfloat16), "grp").astype(jnp.float32),
    )
    left_ready = finish(left_flat, left_coeffs, basis_left, eigen_left).reshape(query_left.shape)
    right_ready = finish(right_flat, right_coeffs, basis_right, eigen_right).reshape(
        query_right.shape
    )
    slot_count = activations.shape[0]
    pieces = (
        lax.all_gather(left_ready, "blk", axis=0, tiled=True),
        lax.all_gather(right_ready, "blk", axis=0, tiled=True),
    )
    left_piece = pieces[0].reshape(-1, pieces[0].shape[2])
    right_piece = pieces[1].reshape(-1, pieces[1].shape[2])
    new_left = contract(activations, left_piece)
    new_right = contract(output_grads, right_piece)
    member = membership(seq_lengths, slot_count)
    sum_left, sum_right = (
        lax.psum(new_left.astype(jnp.bfloat16), "grp").astype(jnp.float32),
        lax.psum(new_right.astype(jnp.bfloat16), "grp").astype(jnp.float32),
    )
    result = jnp.dot(
        member,
        pair_scores(sum_left, sum_right, query_rank),
        precision=lax.Precision.HIGHEST,
        preferred_element_type=jnp.float32,
    )
    return result


def solution(mesh):
    in_specs = (
        P("blk", "grp"),
        P("blk", "grp"),
        P("blk", None, "grp"),
        P("blk", None, "grp"),
        P("blk", "grp", None),
        P("blk", None),
        P("blk", "grp", None),
        P("blk", None),
        P(),
        P("blk"),
    )
    out_specs = P("blk", None)
    return jax.shard_map(local, mesh=mesh, in_specs=in_specs, out_specs=out_specs, check_vma=False)
```

profile of v0, /device:TPU:1, one launch (start us, length us, event | category | flops | bytes accessed | tf_op | source)
XLA Modules:
  0.0 944.6 jit_solution(18013591543518392698)
XLA Ops:
  6.5 0.0 copy-start
  6.5 1.4 fusion.15
  9.2 0.0 copy-start.2
  9.2 2.1 select_bitcast_fusion
  11.3 0.9 select_bitcast_fusion.1
  12.2 0.0 all-reduce.9.cloned.1.call-update
  12.2 0.0 all-reduce.7.cloned.1.call-start
  12.3 0.0 copy-done.6
  12.4 70.3 %all-reduce = (bf16[512]{0:T(512)(128)(2,1)S(1)}, bf16[256]{0:T(256)(128)(2,1)S(1)}) all-reduce(bf16[512]{0:T(512)(128)(2,1)S(1)} %fusion.13, bf16[256]{0:T(256)(128)(2,1)S(1)} %fusion.14), channel_id=1, replica_groups=mesh['blk'=32,'grp'=8] {'blk'}, use_global_device_ids=true, to_apply=%region_7.8 | all-reduce | flops 768 | bytes 3072 | tf_op jit(solution)/shard_map/psum | solution.py:9
  82.7 227.5 %all-reduce.9.cloned.1.call-done = (bf16[3584,512]{1,0:T(8,128)(2,1)}, bf16[1024,256]{1,0:T(8,128)(2,1)}) async-done(((bf16[3584,512]{1,0:T(8,128)(2,1)}, bf16[1024,256]{1,0:T(8,128)(2,1)}), (bf16[3584,512]{1,0:T(8,128)(2,1)}, bf16[1024,256]{1,0:T(8,128)(2,1)})) %all-reduce.9.cloned.1.call-update) | async-done | bytes 4194320 | tf_op jit(solution)/shard_map/psum | solution.py:9
  310.2 3.9 fusion.4
  314.1 0.0 all-reduce.7.cloned.1.call-update
  314.2 0.0 all-gather.3.cloned.1.call-start
  314.2 0.3 fusion.5
  314.6 44.7 %psum.57 = bf16[64,256]{0,1:T(8,128)(2,1)S(1)} all-reduce(bf16[64,256]{0,1:T(8,128)(2,1)S(1)} %fusion.5), channel_id=1, replica_groups=mesh['blk'=32,'grp'=8] {'grp'}, use_global_device_ids=true, to_apply=%region_2.3 | all-reduce | flops 16384 | bytes 65536 | tf_op jit(solution)/shard_map/psum | solution.py:63
  359.3 1.0 fusion.3
  360.3 0.0 all-gather.3.cloned.1.call-update
  360.3 0.0 all-gather.5.cloned.1.call-start
  360.4 53.4 %all-reduce.7.cloned.1.call-done = bf16[64,512]{0,1:T(8,128)(2,1)} async-done(((bf16[64,512]{0,1:T(8,128)(2,1)}), bf16[64,512]{0,1:T(8,128)(2,1)}) %all-reduce.7.cloned.1.call-update) | async-done | bytes 65552 | tf_op jit(solution)/shard_map/psum | solution.py:64
  413.7 4.3 fusion
  418.0 0.0 all-gather.5.cloned.1.call-update
  418.0 0.0 all-reduce.11.cloned.1.call-start
  418.1 60.6 %all-gather.3.cloned.1.call-done = bf16[64,32,1024]{2,1,0:T(8,128)(2,1)} async-done(((bf16[2,32,1024]{2,1,0:T(8,128)(2,1)}), bf16[64,32,1024]{2,1,0:T(8,128)(2,1)}) %all-gather.3.cloned.1.call-update) | async-done | bytes 4194320 | tf_op jit(solution)/shard_map/all_gather | solution.py:72
  478.6 5.9 fusion.2
  484.5 83.8 %all-gather.5.cloned.1.call-done = bf16[64,32,3584]{2,1,0:T(8,128)(2,1)} async-done(((bf16[2,32,3584]{2,1,0:T(8,128)(2,1)}), bf16[64,32,3584]{2,1,0:T(8,128)(2,1)}) %all-gather.5.cloned.1.call-update) | async-done | bytes 14680080 | tf_op jit(solution)/shard_map/all_gather | solution.py:73
  568.3 13.1 %fusion.1 = bf16[512,2048]{0,1:T(8,128)(2,1)} fusion(bf16[2048,3584]{1,0:T(8,128)(2,1)} %bitcast.43, bf16[512,3584]{1,0:T(8,128)(2,1)} %param.11), kind=kOutput, calls=%fused_computation.7 | convolution fusion | flops 7517241344 | bytes 20447232 | tf_op jit(solution)/shard_map/dot_general | solution.py:13
  581.4 0.0 all-reduce.11.cloned.1.call-update
  581.4 0.6 copy-done.7
  582.1 0.2 reduce-window.8
  582.2 351.7 %all-reduce.11.cloned.1.call-done = (bf16[512,2048]{0,1:T(8,128)(2,1)}, bf16[512,2048]{0,1:T(8,128)(2,1)}) async-done(((bf16[512,2048]{0,1:T(8,128)(2,1)}, bf16[512,2048]{0,1:T(8,128)(2,1)}), (bf16[512,2048]{0,1:T(8,128)(2,1)}, bf16[512,2048]{0,1:T(8,128)(2,1)})) %all-reduce.11.cloned.1.call-update) | async-done | bytes 4194320 | tf_op jit(solution)/shard_map/psum | solution.py:82
  934.0 3.3 bitcast_reduce_fusion
  937.2 0.8 fusion.9
  (18 shorter events, 0.1 us)
Async XLA Ops:
  6.5 472.1 %copy-start = (bf16[512,1024]{1,0:T(8,128)(2,1)S(1)}, bf16[512,1024]{1,0:T(8,128)(2,1)}, u32[]{:S(2)}) copy-start(bf16[512,1024]{1,0:T(8,128)(2,1)} %param.10) | copy-start | bytes 3145732
  6.5 303.7 %all-reduce.9.cloned.1.call-start = ((), (), s32[]{:S(2)}) async-start(), calls=%async_computation.3 | async-start | bytes 8388608 | tf_op jit(solution)/shard_map/psum | solution.py:9
  9.2 2.1 copy-start.2
  11.3 1.0 copy-start.6
  11.3 1.0 copy-start.5
  11.3 298.9 %copy-start.4 = (bf16[2,32,3584]{2,1,0:T(8,128)(2,1)S(1)}, bf16[2,32,3584]{2,1,0:T(8,128)(2,1)}, u32[]{:S(2)}) copy-start(bf16[2,32,3584]{2,1,0:T(8,128)(2,1)} %param.13) | copy-start | bytes 1376260
  12.2 302.0 %copy-start.3 = (bf16[2,32,1024]{2,1,0:T(8,128)(2,1)S(1)}, bf16[2,32,1024]{2,1,0:T(8,128)(2,1)}, u32[]{:S(2)}) copy-start(bf16[2,32,1024]{2,1,0:T(8,128)(2,1)} %param.12) | copy-start | bytes 393220
  12.2 401.5 %all-reduce.7.cloned.1.call-start = ((), (), s32[]{:S(2)}) async-start(), calls=%async_computation.1 | async-start | bytes 262144 | tf_op jit(solution)/shard_map/psum | solution.py:64
  310.2 4.0 copy-start.1
  314.2 164.5 %all-gather.3.cloned.1.call-start = ((), (), s32[]{:S(2)}) async-start(), calls=%async_computation | async-start | bytes 4325376 | tf_op jit(solution)/shard_map/all_gather | solution.py:72
  360.3 208.0 %all-gather.5.cloned.1.call-start = ((), (), s32[]{:S(2)}) async-start(), calls=%async_computation.2 | async-start | bytes 15138816 | tf_op jit(solution)/shard_map/all_gather | solution.py:73
  418.0 515.9 %all-reduce.11.cloned.1.call-start = ((), (), s32[]{:S(2)}) async-start(), calls=%async_computation.4 | async-start | bytes 8388608 | tf_op jit(solution)/shard_map/psum | solution.py:82
  581.4 0.7 copy-start.7
Sparse Core Ops, SparseCore 0:
  12.4 297.7 all-reduce.8
  314.3 99.4 all-reduce.6
  415.6 62.9 all-gather.2
  480.3 87.9 all-gather.4
  581.5 352.3 all-reduce.10
where the time goes:
time: 945 us
  waiting for transfers between devices  777 us (82%)
  blocking collectives  115 us (12%)
  matrix products  29.3 us (3%)
  between operations  14.5 us (2%)
    psum x1, waiting for transfers between devices, local(): lax.psum(new_right.astype(jnp.bfloat16), 'grp').astype(jnp.float32)  352 us
    psum x1, waiting for transfers between devices, broadcast(): return lax.psum(jnp.where(mine, x, jnp.zeros_like(x)), axis)  228 us
    all_gather x1, waiting for transfers between devices, local(): lax.all_gather(right_ready, 'blk', axis=0, tiled=True)  83.8 us
    psum x1, blocking collectives, broadcast(): return lax.psum(jnp.where(mine, x, jnp.zeros_like(x)), axis)  70.3 us
    all_gather x1, waiting for transfers between devices, local(): lax.all_gather(left_ready, 'blk', axis=0, tiled=True)  60.6 us
    psum x1, waiting for transfers between devices, local(): lax.psum(right_coeffs.astype(jnp.bfloat16), 'grp').astype(jnp.float32)  53.4 us
    psum x1, blocking collectives, local(): lax.psum(left_coeffs.astype(jnp.bfloat16), 'grp').astype(jnp.float32)  44.7 us
    dot_general x4, matrix products, contract(): lax.dot_general(row_block, factors, (((1,), (1,)), ((), ())), preferred_e...  24.2 us
  transfers between devices with their start and end apart: 5, of which 5 were waited for; matrix products, arithmetic and copies ran while one was open for 1% of the time, Pallas kernels for 0%

commit v1 on v0

--- a/solution.py
+++ b/solution.py
@@ -2,6 +2,13 @@
 import jax.numpy as jnp
 from jax import lax
 from jax.sharding import PartitionSpec as P
+
+
+def all_by_exchange(block, mesh_axis, d):
+    n_dev = lax.axis_size(mesh_axis)
+    pieces = jnp.stack([block for _ in range(n_dev)])
+    pieces = lax.all_to_all(pieces, mesh_axis, split_axis=0, concat_axis=0)
+    return jnp.concatenate(pieces, axis=d)
 
 
 def broadcast(x, axis, root):
@@ -70,7 +77,7 @@
     slot_count = activations.shape[0]
     pieces = (
         lax.all_gather(left_ready, "blk", axis=0, tiled=True),
-        lax.all_gather(right_ready, "blk", axis=0, tiled=True),
+        all_by_exchange(right_ready, "blk", 0),
     )
     left_piece = pieces[0].reshape(-1, pieces[0].shape[2])
     right_piece = pieces[1].reshape(-1, pieces[1].shape[2])

time: 945 us -> 1170 us (1.24)
  blocking collectives: 115 us -> 349 us
  waiting for transfers between devices: 777 us -> 754 us
    psum x1, blocking collectives: 44.7 us -> 279 us  [local(): lax.psum(left_coeffs.astype(jnp.bfloat16), 'grp').astype(jnp.float32)]
    all_gather x1 -> x0, waiting for transfers between devices: 83.8 us -> none  [local(): lax.all_gather(right_ready, 'blk', axis=0, tiled=True)]
    psum x1, waiting for transfers between devices: 53.4 us -> 99.5 us  [local(): lax.psum(right_coeffs.astype(jnp.bfloat16), 'grp').astype(jnp.float32)]
    all_gather x1, waiting for transfers between devices: 60.6 us -> 77.5 us  [local(): lax.all_gather(left_ready, 'blk', axis=0, tiled=True)]
  transfers between devices with their start and end apart: 5 -> 5, of which waited for: 5 -> 4; matrix products, arithmetic and copies ran while one was open for 1% -> 1% of each run, Pallas kernels for 0% -> 0%
where the time goes in v1:
time: 1170 us
  waiting for transfers between devices  754 us (64%)
  blocking collectives  349 us (30%)
  matrix products  28.5 us (2%)
  between operations  14.5 us (1%)
    psum x1, waiting for transfers between devices, local(): lax.psum(new_right.astype(jnp.bfloat16), 'grp').astype(jnp.float32)  349 us
    psum x1, blocking collectives, local(): lax.psum(left_coeffs.astype(jnp.bfloat16), 'grp').astype(jnp.float32)  279 us
    psum x1, waiting for transfers between devices, broadcast(): return lax.psum(jnp.where(mine, x, jnp.zeros_like(x)), axis)  228 us
    psum x1, waiting for transfers between devices, local(): lax.psum(right_coeffs.astype(jnp.bfloat16), 'grp').astype(jnp.float32)  99.5 us
    all_gather x1, waiting for transfers between devices, local(): lax.all_gather(left_ready, 'blk', axis=0, tiled=True)  77.5 us
    psum x1, blocking collectives, broadcast(): return lax.psum(jnp.where(mine, x, jnp.zeros_like(x)), axis)  70.3 us
    dot_general x4, matrix products, contract(): lax.dot_general(row_block, factors, (((1,), (1,)), ((), ())), preferred_e...  23.5 us
  transfers between devices with their start and end apart: 5, of which 4 were waited for; matrix products, arithmetic and copies ran while one was open for 1% of the time, Pallas kernels for 0%

profile of v1, /device:TPU:1, one launch (start us, length us, event | category | flops | bytes accessed | tf_op | source)
XLA Modules:
  0.0 1172.2 jit_solution(6634707646758219344)
XLA Ops:
  6.5 0.0 copy-start
  6.5 1.4 fusion.15
  9.2 0.0 copy-start.2
  9.2 2.1 select_bitcast_fusion
  11.3 0.8 select_bitcast_fusion.1
  12.1 0.0 all-reduce.9.cloned.1.call-update
  12.2 0.0 all-reduce.7.cloned.1.call-start
  12.3 70.3 %all-reduce = (bf16[512]{0:T(512)(128)(2,1)S(1)}, bf16[256]{0:T(256)(128)(2,1)S(1)}) all-reduce(bf16[512]{0:T(512)(128)(2,1)S(1)} %fusion.13, bf16[256]{0:T(256)(128)(2,1)S(1)} %fusion.14), channel_id=1, replica_groups=mesh['blk'=32,'grp'=8] {'blk'}, use_global_device_ids=true, to_apply=%region_7.8 | all-reduce | flops 768 | bytes 3072 | tf_op jit(solution)/shard_map/psum | solution.py:16
  82.6 227.5 %all-reduce.9.cloned.1.call-done = (bf16[3584,512]{1,0:T(8,128)(2,1)}, bf16[1024,256]{1,0:T(8,128)(2,1)}) async-done(((bf16[3584,512]{1,0:T(8,128)(2,1)}, bf16[1024,256]{1,0:T(8,128)(2,1)}), (bf16[3584,512]{1,0:T(8,128)(2,1)}, bf16[1024,256]{1,0:T(8,128)(2,1)})) %all-reduce.9.cloned.1.call-update) | async-done | bytes 4194320 | tf_op jit(solution)/shard_map/psum | solution.py:16
  310.1 0.0 copy-done.4
  310.1 3.8 fusion.4
  314.0 0.0 all-reduce.7.cloned.1.call-update
  314.0 99.5 %all-reduce.7.cloned.1.call-done = bf16[64,512]{0,1:T(8,128)(2,1)} async-done(((bf16[64,512]{0,1:T(8,128)(2,1)}), bf16[64,512]{0,1:T(8,128)(2,1)}) %all-reduce.7.cloned.1.call-update) | async-done | bytes 65552 | tf_op jit(solution)/shard_map/psum | solution.py:71
  413.5 3.5 fusion
  417.0 7.0 stack.3
  424.0 11.0 all-to-all-start
  435.0 0.0 all-gather.2.cloned.1.call-start
  435.1 0.3 fusion.5
  435.4 278.8 %psum.57 = bf16[64,256]{0,1:T(8,128)(2,1)S(1)} all-reduce(bf16[64,256]{0,1:T(8,128)(2,1)S(1)} %fusion.5), channel_id=1, replica_groups=mesh['blk'=32,'grp'=8] {'grp'}, use_global_device_ids=true, to_apply=%region_2.3 | all-reduce | flops 16384 | bytes 65536 | tf_op jit(solution)/shard_map/psum | solution.py:70
  714.3 1.0 fusion.3
  715.3 0.0 all-gather.2.cloned.1.call-update
  715.3 0.0 all-reduce.11.cloned.1.call-start
  715.4 77.5 %all-gather.2.cloned.1.call-done = bf16[64,32,1024]{2,1,0:T(8,128)(2,1)} async-done(((bf16[2,32,1024]{2,1,0:T(8,128)(2,1)}), bf16[64,32,1024]{2,1,0:T(8,128)(2,1)}) %all-gather.2.cloned.1.call-update) | async-done | bytes 4194320 | tf_op jit(solution)/shard_map/all_gather | solution.py:79
  792.8 5.9 fusion.2
  798.7 0.0 all-to-all-done
  798.7 13.1 %fusion.1 = bf16[512,2048]{0,1:T(8,128)(2,1)} fusion(bf16[2048,3584]{1,0:T(8,128)(2,1)} %bitcast.14, bf16[512,3584]{1,0:T(8,128)(2,1)} %param.11), kind=kOutput, calls=%fused_computation.7 | convolution fusion | flops 7517241344 | bytes 20447232 | tf_op jit(solution)/shard_map/dot_general | solution.py:20
  811.8 0.0 all-reduce.11.cloned.1.call-update
  811.8 0.6 copy-done.7
  812.5 0.2 reduce-window.8
  812.7 348.9 %all-reduce.11.cloned.1.call-done = (bf16[512,2048]{0,1:T(8,128)(2,1)}, bf16[512,2048]{0,1:T(8,128)(2,1)}) async-done(((bf16[512,2048]{0,1:T(8,128)(2,1)}, bf16[512,2048]{0,1:T(8,128)(2,1)}), (bf16[512,2048]{0,1:T(8,128)(2,1)}, bf16[512,2048]{0,1:T(8,128)(2,1)})) %all-reduce.11.cloned.1.call-update) | async-done | bytes 4194320 | tf_op jit(solution)/shard_map/psum | solution.py:89
  1161.6 3.3 bitcast_reduce_fusion
  1164.9 0.8 fusion.9
  (18 shorter events, 0.1 us)
Async XLA Ops:
  6.5 786.3 %copy-start = (bf16[512,1024]{1,0:T(8,128)(2,1)S(1)}, bf16[512,1024]{1,0:T(8,128)(2,1)}, u32[]{:S(2)}) copy-start(bf16[512,1024]{1,0:T(8,128)(2,1)} %param.10) | copy-start | bytes 3145732
  6.5 303.6 %all-reduce.9.cloned.1.call-start = ((), (), s32[]{:S(2)}) async-start(), calls=%async_computation.3 | async-start | bytes 8388608 | tf_op jit(solution)/shard_map/psum | solution.py:16
  9.2 2.1 copy-start.2
  11.3 0.9 copy-start.6
  11.3 0.9 copy-start.5
  11.3 298.8 %copy-start.4 = (bf16[2,32,3584]{2,1,0:T(8,128)(2,1)S(1)}, bf16[2,32,3584]{2,1,0:T(8,128)(2,1)}, u32[]{:S(2)}) copy-start(bf16[2,32,3584]{2,1,0:T(8,128)(2,1)} %param.13) | copy-start | bytes 1376260
  12.2 401.4 %all-reduce.7.cloned.1.call-start = ((), (), s32[]{:S(2)}) async-start(), calls=%async_computation.2 | async-start | bytes 262144 | tf_op jit(solution)/shard_map/psum | solution.py:71
  424.0 11.1 copy-start.1
  424.0 11.1 copy-start.3
  424.0 374.8 %all-to-all-start = ((bf16[32,2,32,3584]{3,2,1,0:T(8,128)(2,1)}), bf16[32,2,32,3584]{3,2,1,0:T(8,128)(2,1)}, u32[]{:S(2)}, u32[]{:S(2)}) async-start(bf16[32,2,32,3584]{3,2,1,0:T(8,128)(2,1)} %stack.3), calls=%async_computation | async-start | bytes 29360128 | tf_op jit(solution)/shard_map/all_to_all | solution.py:10
  435.0 357.8 %all-gather.2.cloned.1.call-start = ((), (), s32[]{:S(2)}) async-start(), calls=%async_computation.1 | async-start | bytes 4325376 | tf_op jit(solution)/shard_map/all_gather | solution.py:79
  715.3 446.3 %all-reduce.11.cloned.1.call-start = ((), (), s32[]{:S(2)}) async-start(), calls=%async_computation.4 | async-start | bytes 8388608 | tf_op jit(solution)/shard_map/psum | solution.py:89
  811.8 0.7 copy-start.7
Sparse Core Ops, SparseCore 0:
  12.3 297.7 all-reduce.8
  314.1 99.3 all-reduce.6
  715.4 77.3 all-gather.1
  812.0 349.5 all-reduce.10
